TPU v7x, 32 devices: a whole 2x2x4 slice. The times are simulated.
32 devices in a mesh: dp: 2 (over x), space: 16 (over z, y, core).
Axes of the slice: x: 2, y: 2, z: 4, core: 2. Of those that a mesh axis runs over, the one named last changes fastest.
Arguments:
- stash: bfloat16 [16, 16, 4, 8640], P('space', None, 'dp'), may hold values from -5 to 5
- piece_map: int32 [16, 16], P(None, 'space'), may hold values from 0 to 15, as said below
- gain_one: float32 [768], replicated, may hold values from 0.5 to 1.5
- spec_one: float32 [2, 8, 96, 96], replicated, may hold values from -0.4375 to 0.4375
- bias_one: float32 [2, 768], replicated, may hold values from -3 to 3
- spec_two: float32 [2, 8, 96, 96], replicated, may hold values from -0.4375 to 0.4375
- bias_two: float32 [2, 768], replicated, may hold values from -0.6 to 0.6
- gain_two: float32 [768], replicated, may hold values from 0.5 to 1.5
- fc_one: bfloat16 [768, 3072], replicated, may hold values from -0.21875 to 0.21875
- bias_fc: float32 [3072], replicated, may hold values from -3 to 3
- fc_two: bfloat16 [3072, 768], replicated, may hold values from -0.109375 to 0.109375
- cotangent: bfloat16 [4, 16, 180, 768], P('dp', 'space'), may hold values from -6 to 6
Outputs:
- grad_input: float32 [4, 16, 180, 768], P('dp', 'space')
- grad_fc_one: float32 [768, 3072], P(None, ('dp', 'space'))
- grad_fc_two: float32 [3072, 768], P(('dp', 'space'))
- grad_bias_fc: float32 [3072], replicated
- grad_bias_out: float32 [768], replicated
- grad_gain_one: float32 [768], replicated
- grad_gain_two: float32 [768], replicated
- grad_spec_one: float32 [2, 8, 96, 96], replicated
- grad_bias_one: float32 [2, 768], replicated
- grad_spec_two: float32 [2, 8, 96, 96], replicated
- grad_bias_two: float32 [2, 768], replicated
Inputs may be any that keep to these rules, and one draw needn't show every extreme that they name: `piece_map`: each column holds every number from 0 to 15 once.
All inputs are finite; a program needn't handle non-finite values.
Results may differ from a plain program's by a relative error of at most 0.0046.
Values may be sent and summed in bfloat16 or wider, within the bound.
A program may use at most 128 MiB of HBM per device.

v0:
```python
import math
import jax
import jax.numpy as jnp
from jax import lax
from jax.sharding import PartitionSpec as P

KW = 64
epsilon = 1e-05
highest = lax.Precision.HIGHEST


def layer_norm(values, gain_vector):
    centred = values - jnp.mean(values, axis=-1, keepdims=True)
    spread = jnp.mean(centred * centred, axis=-1, keepdims=True)
    return centred * lax.rsqrt(spread + epsilon) * gain_vector


def smooth_gate(values):
    return jax.nn.gelu(values, approximate=True)


def block_mix(real_part, imag_part, weights, biases):
    blocks = weights.shape[1]
    width_block = weights.shape[2]
    leading = real_part.shape[:-1]
    real_blocks = real_part.reshape(leading + (blocks, width_block))
    imag_blocks = imag_part.reshape(leading + (blocks, width_block))
    bias_real = biases[0].reshape(blocks, width_block)
    bias_imag = biases[1].reshape(blocks, width_block)
    new_real = (
        jnp.einsum("...ni,nio->...no", real_blocks, weights[0], precision=highest)
        - jnp.einsum("...ni,nio->...no", imag_blocks, weights[1], precision=highest)
        + bias_real
    )
    new_imag = (
        jnp.einsum("...ni,nio->...no", real_blocks, weights[1], precision=highest)
        + jnp.einsum("...ni,nio->...no", imag_blocks, weights[0], precision=highest)
        + bias_imag
    )
    return (
        new_real.reshape(leading + (blocks * width_block,)),
        new_imag.reshape(leading + (blocks * width_block,)),
    )


def spectral_mlp(spec_real, spec_imag, spec_one, bias_one, spec_two, bias_two):
    inner_real, inner_imag = block_mix(spec_real, spec_imag, spec_one, bias_one)
    return block_mix(smooth_gate(inner_real), smooth_gate(inner_imag), spec_two, bias_two)


def wave_tables(length, total_modes):
    positions = jnp.arange(length, dtype=jnp.int32)
    frequency = jnp.arange(total_modes, dtype=jnp.int32)
    phases = positions[:, None] * frequency[None, :] % length
    angles = phases.astype(jnp.float32) * (2.0 * math.pi / length)
    factor = 1.0 / math.sqrt(length)
    return (jnp.cos(angles) * factor, jnp.sin(angles) * factor)


def meridian_apply(table, field):
    return jnp.einsum("hk,bhmd->bkmd", table, field, precision=highest)


def meridian_forward(real_part, imag_part, merid_cos, merid_sin):
    new_real = meridian_apply(merid_cos, real_part) + meridian_apply(merid_sin, imag_part)
    new_imag = meridian_apply(merid_cos, imag_part) - meridian_apply(merid_sin, real_part)
    return (new_real, new_imag)


def meridian_inverse(real_part, imag_part, merid_cos, merid_sin):
    new_real = meridian_apply(merid_cos, real_part) - meridian_apply(merid_sin, imag_part)
    new_imag = meridian_apply(merid_cos, imag_part) + meridian_apply(merid_sin, real_part)
    return (new_real, new_imag)


def zonal_project(field, table):
    return jnp.einsum("brwd,wk->brkd", field, table, precision=highest)


def zonal_expand(field, table):
    return jnp.einsum("brkd,wk->brwd", field, table, precision=highest)


def local(
    stash,
    piece_map,
    gain_one,
    spec_one,
    bias_one,
    spec_two,
    bias_two,
    gain_two,
    fc_one,
    bias_fc,
    fc_two,
    cotangent,
):
    samples, lat_rows, lon_cells, model_width = cotangent.shape
    space_ranks = lax.axis_size("space")
    lat_total = lat_rows * space_ranks
    tokens = samples * lat_rows * lon_cells
    arrived = lax.all_to_all(stash, "space", split_axis=1, concat_axis=0, tiled=True)
    ordering = jnp.argsort(piece_map[:, 0])
    placed = jnp.take(arrived[:, 0], ordering, axis=0)
    inputs = jnp.transpose(placed, (1, 0, 2)).reshape(samples, lat_rows, lon_cells, model_width)
    base_field = inputs.astype(jnp.float32)
    zonal_cos, zonal_sin = wave_tables(lon_cells, KW)
    doubling = jnp.where(jnp.arange(KW) == 0, 1.0, 2.0).astype(jnp.float32)
    back_cos = zonal_cos * doubling
    back_sin = zonal_sin * doubling
    merid_cos, merid_sin = wave_tables(lat_total, lat_total)
    normed, pull_one = jax.vjp(layer_norm, base_field, gain_one)
    zonal_real = zonal_project(normed, zonal_cos)
    zonal_imag = -zonal_project(normed, zonal_sin)
    modes_real, modes_imag = (
        lax.all_to_all(zonal_real, "space", split_axis=2, concat_axis=1, tiled=True),
        lax.all_to_all(zonal_imag, "space", split_axis=2, concat_axis=1, tiled=True),
    )
    spec_real, spec_imag = meridian_forward(modes_real, modes_imag, merid_cos, merid_sin)
    mixed_spec, pull_mix = jax.vjp(
        spectral_mlp, spec_real, spec_imag, spec_one, bias_one, spec_two, bias_two
    )
    back_real, back_imag = meridian_inverse(mixed_spec[0], mixed_spec[1], merid_cos, merid_sin)
    rows_real, rows_imag = (
        lax.all_to_all(back_real, "space", split_axis=1, concat_axis=2, tiled=True),
        lax.all_to_all(back_imag, "space", split_axis=1, concat_axis=2, tiled=True),
    )
    spatial = zonal_expand(rows_real, back_cos) - zonal_expand(rows_imag, back_sin)
    mixed_field = base_field + normed + spatial
    normed_two, pull_two = jax.vjp(layer_norm, mixed_field, gain_two)
    normed_flat = normed_two.astype(jnp.bfloat16).reshape(tokens, model_width)
    hidden_pre = jnp.dot(normed_flat, fc_one, preferred_element_type=jnp.float32) + bias_fc
    active, pull_gate = jax.vjp(smooth_gate, hidden_pre)
    active_flat = active.astype(jnp.bfloat16)
    upstream = cotangent.reshape(tokens, model_width)
    grad_active = jnp.einsum("td,fd->tf", upstream, fc_two, preferred_element_type=jnp.float32)
    grad_hidden = pull_gate(grad_active)[0]
    grad_hidden_flat = grad_hidden.astype(jnp.bfloat16)
    grad_normed_two = jnp.einsum(
        "tf,df->td", grad_hidden_flat, fc_one, preferred_element_type=jnp.float32
    )
    term_one = jnp.einsum(
        "td,tf->df", normed_flat, grad_hidden_flat, preferred_element_type=jnp.float32
    )
    term_two = jnp.einsum("td,tf->df", upstream, active_flat, preferred_element_type=jnp.float32)
    grad_mixed_norm, grad_gain_two = pull_two(grad_normed_two.reshape(mixed_field.shape))
    grad_mixed = cotangent.astype(jnp.float32) + grad_mixed_norm
    grad_back_real = zonal_project(grad_mixed, back_cos)
    grad_back_imag = -zonal_project(grad_mixed, back_sin)
    grad_modes_real, grad_modes_imag = (
        lax.all_to_all(grad_back_real, "space", split_axis=2, concat_axis=1, tiled=True),
        lax.all_to_all(grad_back_imag, "space", split_axis=2, concat_axis=1, tiled=True),
    )
    grad_out_real, grad_out_imag = meridian_forward(
        grad_modes_real, grad_modes_imag, merid_cos, merid_sin
    )
    pulled = pull_mix((grad_out_real, grad_out_imag))
    grad_merid_real, grad_merid_imag = meridian_inverse(pulled[0], pulled[1], merid_cos, merid_sin)
    grad_rows_real, grad_rows_imag = (
        lax.all_to_all(grad_merid_real, "space", split_axis=1, concat_axis=2, tiled=True),
        lax.all_to_all(grad_merid_imag, "space", split_axis=1, concat_axis=2, tiled=True),
    )
    grad_normed = (
        grad_mixed
        + zonal_expand(grad_rows_real, zonal_cos)
        - zonal_expand(grad_rows_imag, zonal_sin)
    )
    grad_base, grad_gain_one = pull_one(grad_normed)
    grad_input = grad_mixed + grad_base
    bias_sum = jnp.sum(grad_hidden, axis=0)
    out_sum = jnp.sum(cotangent, axis=(0, 1, 2), dtype=jnp.float32)
    totals = lax.psum(
        (
            grad_gain_one,
            grad_gain_two,
            pulled[2],
            pulled[3],
            pulled[4],
            pulled[5],
            bias_sum,
            out_sum,
        ),
        ("dp", "space"),
    )
    paired = (
        lax.psum_scatter(term_one, "dp", scatter_dimension=1, tiled=True),
        lax.psum_scatter(term_two, "dp", scatter_dimension=1, tiled=True),
    )
    summed = (
        lax.psum_scatter(paired[0], "space", scatter_dimension=1, tiled=True),
        lax.psum_scatter(paired[1], "space", scatter_dimension=1, tiled=True),
    )
    grad_scale = 1.0 / math.sqrt(samples * lax.axis_size("dp") * lat_total * lon_cells)
    return (
        grad_input,
        summed[0] * grad_scale,
        (summed[1] * grad_scale).T,
        totals[6] * grad_scale,
        totals[7] * grad_scale,
        totals[0] * grad_scale,
        totals[1] * grad_scale,
        totals[2] * grad_scale,
        totals[3] * grad_scale,
        totals[4] * grad_scale,
        totals[5] * grad_scale,
    )


def solution(mesh):
    placed = (
        P("space", None, "dp", None),
        P(None, "space"),
        P(),
        P(),
        P(),
        P(),
        P(),
        P(),
        P(),
        P(),
        P(),
        P("dp", "space", None, None),
    )
    return jax.shard_map(
        local,
        mesh=mesh,
        in_specs=placed,
        out_specs=(
            P("dp", "space", None, None),
            P(None, ("dp", "space")),
            P(("dp", "space"), None),
            P(),
            P(),
            P(),
            P(),
            P(),
            P(),
            P(),
            P(),
        ),
        check_vma=False,
    )
```

profile of v0, /device:TPU:0, one launch (start us, length us, event | category | flops | bytes accessed | tf_op | source)
XLA Modules:
  0.0 540.8 jit_solution(15111530025571040540)
XLA Ops:
  8.0 7.4 %all-to-all-start = ((bf16[1,16,2,8640]{3,2,0,1:T(2,128)(2,1)}), bf16[1,16,2,8640]{3,2,0,1:T(2,128)(2,1)S(1)}, u32[]{:S(2)}, u32[]{:S(2)}) async-start(bf16[1,16,2,8640]{3,2,0,1:T(2,128)(2,1)} %bitcast.441), calls=%async_computation | async-start | bytes 1114112 | tf_op jit(solution)/shard_map/all_to_all | solution.py:102
  15.5 1.9 sort.17
  17.4 12.9 %all-to-all-done = bf16[1,16,2,8640]{3,2,0,1:T(2,128)(2,1)S(1)} async-done(((bf16[1,16,2,8640]{3,2,0,1:T(2,128)(2,1)}), bf16[1,16,2,8640]{3,2,0,1:T(2,128)(2,1)S(1)}, u32[]{:S(2)}, u32[]{:S(2)}) %all-to-all-start) | async-done | bytes 552992 | tf_op jit(solution)/shard_map/all_to_all | solution.py:102
  30.2 1.7 gather_fusion
  34.9 1.2 convolution_bitcast_fusion.4
  37.2 4.3 all-to-all-start.1
  41.6 1.3 fusion.29
  43.9 9.8 %all-to-all-done.1 = f32[2,1,64,768]{3,0,1,2:T(2,128)S(1)} async-done(((f32[2,1,64,768]{3,0,1,2:T(2,128)}), f32[2,1,64,768]{3,0,1,2:T(2,128)S(1)}, u32[]{:S(2)}, u32[]{:S(2)}) %all-to-all-start.1) | async-done | bytes 393248 | tf_op jit(solution)/shard_map/all_to_all | solution.py:116
  53.7 4.0 all-to-all-start.2
  58.1 1.3 fusion.143
  59.5 10.4 %all-to-all-done.2 = f32[2,1,64,768]{3,0,1,2:T(2,128)S(1)} async-done(((f32[2,1,64,768]{3,0,1,2:T(2,128)}), f32[2,1,64,768]{3,0,1,2:T(2,128)S(1)}, u32[]{:S(2)}, u32[]{:S(2)}) %all-to-all-start.2) | async-done | bytes 393248 | tf_op jit(solution)/shard_map/all_to_all | solution.py:117
  69.9 1.3 fusion.139
  71.2 1.6 fusion.28
  73.8 1.5 fusion.106
  75.3 1.3 fusion.27
  76.6 1.3 reshape.375
  80.1 1.6 fusion.111
  84.3 1.8 fusion.19
  88.7 3.7 all-to-all-start.3
  95.5 9.1 %all-to-all-done.3 = f32[2,16,4,768]{3,2,0,1:T(4,128)S(1)} async-done(((f32[2,16,4,768]{3,2,0,1:T(4,128)}), f32[2,16,4,768]{3,2,0,1:T(4,128)S(1)}, u32[]{:S(2)}, u32[]{:S(2)}) %all-to-all-start.3) | async-done | bytes 393248 | tf_op jit(solution)/shard_map/all_to_all | solution.py:125
  104.5 3.6 all-to-all-start.4
  108.2 6.3 %fusion.368 = f32[360,3072]{1,0:T(8,128)} fusion(bf16[360,768]{1,0:T(8,128)(2,1)S(1)} %copy-done.24, bf16[3072,768]{1,0:T(8,128)(2,1)} %param.22), kind=kOutput, calls=%fused_computation.459 | convolution fusion | flops 1698693120 | bytes 9695232 | tf_op jit(solution)/shard_map/td,fd->tf/dot_general | solution.py:136
  114.7 1.3 fusion.131
  116.1 4.2 all-to-all-done.4
  120.4 1.6 fusion.365
  123.4 9.3 %fusion.363 = (f32[3072]{0:T(1024)S(1)}, bf16[360,3072]{1,0:T(8,128)(2,1)S(1)}, f32[360,3072]{1,0:T(8,128)}) fusion(f32[360,3072]{1,0:T(8,128)} %fusion.368, f32[3072]{0:T(1024)S(1)} %copy-done.30, bf16[360,768]{1,0:T(8,128)(2,1)S(1)} %reshape.380, bf16[768,3072]{1,0:T(8,128)(2,1)} %param.20), kind=kOutput, calls=%fused_computation.455 | convolution fusion | flops 1723020288 | bytes 16355328 | tf_op jit(solution)/shard_map/dot_general | solution.py:132
  132.8 1.4 copy-done.17
  134.2 5.1 fusion.32
  140.4 8.9 %convolution_bitcast_fusion = f32[768,3072]{0,1:T(8,128)} fusion(bf16[360,768]{1,0:T(8,128)(2,1)S(1)} %copy-done.25, f32[360,3072]{1,0:T(8,128)} %get-tuple-element.83), kind=kOutput, calls=%fused_computation.3 | convolution fusion | flops 1708646400 | bytes 14413824 | tf_op jit(solution)/shard_map/td,tf->df/dot_general | solution.py:145
  149.3 6.0 %fusion.34 = f32[360,768]{1,0:T(8,128)} fusion(bf16[768,3072]{1,0:T(8,128)(2,1)} %param.20, bf16[360,3072]{1,0:T(8,128)(2,1)} %copy-done.17), kind=kOutput, calls=%fused_computation.86 | convolution fusion | flops 1698693120 | bytes 8036352 | tf_op jit(solution)/shard_map/tf,df->td/dot_general | solution.py:139
  155.2 1.4 reshape.381
  158.6 1.7 convert_reduce_fusion
  162.5 3.7 all-to-all-start.6
  168.4 10.0 %all-to-all-done.6 = f32[2,1,64,768]{3,0,1,2:T(2,128)S(1)} async-done(((f32[2,1,64,768]{3,0,1,2:T(2,128)}), f32[2,1,64,768]{3,0,1,2:T(2,128)S(1)}, u32[]{:S(2)}, u32[]{:S(2)}) %all-to-all-start.6) | async-done | bytes 393248 | tf_op jit(solution)/shard_map/all_to_all | solution.py:151
  178.4 3.6 all-to-all-start.5
  182.4 1.3 fusion.133
  183.7 10.3 %all-to-all-done.5 = f32[2,1,64,768]{3,0,1,2:T(2,128)S(1)} async-done(((f32[2,1,64,768]{3,0,1,2:T(2,128)}), f32[2,1,64,768]{3,0,1,2:T(2,128)S(1)}, u32[]{:S(2)}, u32[]{:S(2)}) %all-to-all-start.5) | async-done | bytes 393248 | tf_op jit(solution)/shard_map/all_to_all | solution.py:152
  194.1 1.6 fusion.366
  197.3 1.3 fusion.367
  198.7 1.3 reshape.383
  200.0 2.0 fusion.87
  202.1 1.2 fusion.61
  211.0 1.2 convolution_bitcast_fusion.6
  216.7 33.6 %reduce-scatter.9.cloned.1.call-done = f32[768,1536]{1,0:T(8,128)} async-done(((f32[768,3072]{1,0:T(8,128)}), f32[768,1536]{1,0:T(8,128)}) %reduce-scatter.9.cloned.1.call-update) | async-done | bytes 4718608 | tf_op jit(solution)/shard_map/reduce_scatter | solution.py:186
  250.3 6.1 %copy.208 = f32[768,1536]{0,1:T(8,128)} copy(f32[768,1536]{1,0:T(8,128)} %reduce-scatter.9.cloned.1.call-done) | data formatting | bytes 9437184
  256.5 108.2 %reduce-scatter.11.cloned.1.call-done = f32[768,1536]{0,1:T(8,128)} async-done(((f32[768,3072]{0,1:T(8,128)}), f32[768,1536]{0,1:T(8,128)}) %reduce-scatter.11.cloned.1.call-update) | async-done | bytes 4718608 | tf_op jit(solution)/shard_map/reduce_scatter | solution.py:187
  364.7 1.1 copy-done.6
  365.9 1.9 fusion.124
  368.6 1.1 copy.171
  369.8 1.2 reshape.385
  371.0 1.9 fusion.118
  374.9 1.3 reshape.386
  378.2 5.6 %all-to-all-start.8 = ((f32[2,16,4,768]{3,2,0,1:T(4,128)}), f32[2,16,4,768]{3,2,0,1:T(4,128)S(1)}, u32[]{:S(2)}, u32[]{:S(2)}) async-start(f32[2,16,4,768]{3,2,0,1:T(4,128)} %copy.176), calls=%async_computation.8 | async-start | bytes 786432 | tf_op jit(solution)/shard_map/all_to_all | solution.py:161
  385.9 10.2 %all-to-all-done.8 = f32[2,16,4,768]{3,2,0,1:T(4,128)S(1)} async-done(((f32[2,16,4,768]{3,2,0,1:T(4,128)}), f32[2,16,4,768]{3,2,0,1:T(4,128)S(1)}, u32[]{:S(2)}, u32[]{:S(2)}) %all-to-all-start.8) | async-done | bytes 393248 | tf_op jit(solution)/shard_map/all_to_all | solution.py:161
  396.2 4.0 all-to-all-start.7
  400.4 43.3 %all-reduce.16.cloned.1.call-done = (f32[2,8,96,96]{3,2,1,0:T(8,128)}, f32[2,8,96,96]{3,2,1,0:T(8,128)}) async-done(((f32[2,8,96,96]{3,2,1,0:T(8,128)}, f32[2,8,96,96]{3,2,1,0:T(8,128)}), (f32[2,8,96,96]{3,2,1,0:T(8,128)}, f32[2,8,96,96]{3,2,1,0:T(8,128)})) %all-reduce.16.cloned.1.call-update) | async-done | bytes 1179664 | tf_op jit(solution)/shard_map/psum | solution.py:172
  443.7 2.7 broadcast_multiply_fusion
  446.8 1.3 convolution_bitcast_fusion.1
  448.2 1.7 multiply_reduce_fusion.2
  450.9 2.1 copy.188
  453.0 41.9 %all-reduce.12 = (f32[3072]{0:T(1024)S(1)}, f32[768]{0:T(1024)S(1)}, f32[768]{0:T(1024)S(1)}, f32[768]{0:T(1024)S(1)}, f32[2,768]{1,0:T(2,128)S(1)}, /*index=5*/f32[2,768]{1,0:T(2,128)S(1)}) all-reduce(f32[3072]{0:T(1024)S(1)} %get-tuple-element.73, ...), channel_id=1, replica_groups=mesh['dp'=2,'space'=16] {'dp','space'}, use_global_device_ids=true, to_apply=%region_14.15 | all-reduce | flops 8448 | bytes 67584 | tf_op jit(solution)/shard_map/psum | solution.py:172
  497.4 1.1 copy.209
  499.4 32.0 %reduce-scatter.15.cloned.1.call-done = f32[96,768]{1,0:T(8,128)} async-done(((f32[1536,768]{1,0:T(8,128)}), f32[96,768]{1,0:T(8,128)}) %reduce-scatter.15.cloned.1.call-update) | async-done | bytes 294928
  531.4 1.1 copy.211
  (170 shorter events, 52.8 us)
Async XLA Ops:
  8.0 22.2 %all-to-all-start = ((bf16[1,16,2,8640]{3,2,0,1:T(2,128)(2,1)}), bf16[1,16,2,8640]{3,2,0,1:T(2,128)(2,1)S(1)}, u32[]{:S(2)}, u32[]{:S(2)}) async-start(bf16[1,16,2,8640]{3,2,0,1:T(2,128)(2,1)} %bitcast.441), calls=%async_computation | async-start | bytes 1114112 | tf_op jit(solution)/shard_map/all_to_all | solution.py:102
  34.3 0.7 copy-start.26
  37.2 16.5 %all-to-all-start.1 = ((f32[2,1,64,768]{3,0,1,2:T(2,128)}), f32[2,1,64,768]{3,0,1,2:T(2,128)S(1)}, u32[]{:S(2)}, u32[]{:S(2)}) async-start(f32[2,1,64,768]{3,0,1,2:T(2,128)} %copy.140), calls=%async_computation.1 | async-start | bytes 786432 | tf_op jit(solution)/shard_map/all_to_all | solution.py:116
  42.8 14.9 %copy-start.28 = (f32[2,768]{1,0:T(2,128)S(1)}, f32[2,768]{1,0:T(2,128)}, u32[]{:S(2)}) copy-start(f32[2,768]{1,0:T(2,128)} %param.16) | copy-start | bytes 18436
  42.8 15.1 %copy-start.29 = (f32[2,768]{1,0:T(2,128)S(1)}, f32[2,768]{1,0:T(2,128)}, u32[]{:S(2)}) copy-start(f32[2,768]{1,0:T(2,128)} %param.18) | copy-start | bytes 18436
  53.7 16.1 %all-to-all-start.2 = ((f32[2,1,64,768]{3,0,1,2:T(2,128)}), f32[2,1,64,768]{3,0,1,2:T(2,128)S(1)}, u32[]{:S(2)}, u32[]{:S(2)}) async-start(f32[2,1,64,768]{3,0,1,2:T(2,128)} %copy.142), calls=%async_computation.2 | async-start | bytes 786432 | tf_op jit(solution)/shard_map/all_to_all | solution.py:117
  71.2 1.9 copy-start.5
  73.2 2.1 copy-start.1
  73.2 2.1 copy-start.23
  76.6 1.3 copy-start.22
  78.0 3.7 copy-start.3
  78.0 1.3 copy-start.14
  79.3 2.4 copy-start.20
  82.3 1.3 copy-start.7
  83.2 1.1 copy-start.15
  87.1 5.3 copy-start.18
  88.7 15.8 %all-to-all-start.3 = ((f32[2,16,4,768]{3,2,0,1:T(4,128)}), f32[2,16,4,768]{3,2,0,1:T(4,128)S(1)}, u32[]{:S(2)}, u32[]{:S(2)}) async-start(f32[2,16,4,768]{3,2,0,1:T(4,128)} %copy.152), calls=%async_computation.3 | async-start | bytes 786432 | tf_op jit(solution)/shard_map/all_to_all | solution.py:125
  94.4 13.7 %copy-start.24 = (bf16[360,768]{1,0:T(8,128)(2,1)S(1)}, bf16[360,768]{1,0:T(8,128)(2,1)}, u32[]{:S(2)}) copy-start(bf16[360,768]{1,0:T(8,128)(2,1)} %reshape.373) | copy-start | bytes 1658884
  104.5 15.7 %all-to-all-start.4 = ((f32[2,16,4,768]{3,2,0,1:T(4,128)}), f32[2,16,4,768]{3,2,0,1:T(4,128)S(1)}, u32[]{:S(2)}, u32[]{:S(2)}) async-start(f32[2,16,4,768]{3,2,0,1:T(4,128)} %copy.155), calls=%async_computation.4 | async-start | bytes 786432 | tf_op jit(solution)/shard_map/all_to_all | solution.py:126
  108.1 142.2 %reduce-scatter.9.cloned.1.call-start = ((), (), s32[]{:S(2)}) async-start(), calls=%async_computation.13 | async-start | bytes 14155776 | tf_op jit(solution)/shard_map/reduce_scatter | solution.py:186
  122.0 0.7 copy-start.27
  122.7 0.7 copy-start.30
  132.8 1.5 copy-start.17
  139.3 1.1 copy-start.25
  139.4 225.4 %reduce-scatter.11.cloned.1.call-start = ((), (), s32[]{:S(2)}) async-start(), calls=%async_computation.14 | async-start | bytes 14155776 | tf_op jit(solution)/shard_map/reduce_scatter | solution.py:187
  156.6 1.0 copy-start
  157.6 1.1 copy-start.19
  162.5 15.9 %all-to-all-start.6 = ((f32[2,1,64,768]{3,0,1,2:T(2,128)}), f32[2,1,64,768]{3,0,1,2:T(2,128)S(1)}, u32[]{:S(2)}, u32[]{:S(2)}) async-start(f32[2,1,64,768]{3,0,1,2:T(2,128)} %copy.160), calls=%async_computation.6 | async-start | bytes 786432 | tf_op jit(solution)/shard_map/all_to_all | solution.py:151
  178.4 15.7 %all-to-all-start.5 = ((f32[2,1,64,768]{3,0,1,2:T(2,128)}), f32[2,1,64,768]{3,0,1,2:T(2,128)S(1)}, u32[]{:S(2)}, u32[]{:S(2)}) async-start(f32[2,1,64,768]{3,0,1,2:T(2,128)} %copy.158), calls=%async_computation.5 | async-start | bytes 786432 | tf_op jit(solution)/shard_map/all_to_all | solution.py:152
  181.9 261.8 %all-reduce.16.cloned.1.call-start = ((), (), s32[]{:S(2)}) async-start(), calls=%async_computation.17 | async-start | bytes 3145728 | tf_op jit(solution)/shard_map/psum | solution.py:172
  198.7 3.4 copy-start.8
  200.0 2.1 copy-start.13
  200.0 2.1 copy-start.16
  202.1 1.2 copy-start.2
  203.3 2.3 copy-start.9
  203.3 1.2 copy-start.4
  204.5 1.9 copy-start.21
  207.5 2.1 copy-start.10
  216.7 280.7 %reduce-scatter.13.cloned.1.call-start = ((), (), s32[]{:S(2)}) async-start(), calls=%async_computation.15 | async-start | bytes 5013504
  256.4 275.0 %reduce-scatter.15.cloned.1.call-start = ((), (), s32[]{:S(2)}) async-start(), calls=%async_computation.16 | async-start | bytes 5013504
  364.7 1.1 copy-start.6
  365.9 1.9 copy-start.11
  371.0 1.9 copy-start.12
  378.2 17.9 %all-to-all-start.8 = ((f32[2,16,4,768]{3,2,0,1:T(4,128)}), f32[2,16,4,768]{3,2,0,1:T(4,128)S(1)}, u32[]{:S(2)}, u32[]{:S(2)}) async-start(f32[2,16,4,768]{3,2,0,1:T(4,128)} %copy.176), calls=%async_computation.8 | async-start | bytes 786432 | tf_op jit(solution)/shard_map/all_to_all | solution.py:161
  396.2 50.4 %all-to-all-start.7 = ((f32[2,16,4,768]{3,2,0,1:T(4,128)}), f32[2,16,4,768]{3,2,0,1:T(4,128)S(1)}, u32[]{:S(2)}, u32[]{:S(2)}) async-start(f32[2,16,4,768]{3,2,0,1:T(4,128)} %copy.173), calls=%async_computation.7 | async-start | bytes 786432 | tf_op jit(solution)/shard_map/all_to_all | solution.py:160
Sparse Core Ops, SparseCore 0:
  139.5 110.7 reduce-scatter.8
  252.6 112.1 reduce-scatter.10
  368.6 83.4 reduce-scatter.12
  455.8 75.5 reduce-scatter.14
Sparse Core Ops, SparseCore 1:
  216.7 226.9 all-reduce.15
where the time goes:
time: 549 us; the launch traced here: 541 us
  waiting for transfers between devices  294 us (54%)
  matrix products  88.4 us (16%)
  local copies, waits for them, and re-layouts  44.3 us (8%)
  blocking collectives  41.9 us (8%)
  starting transfers between devices  40.8 us (7%)
  between operations  16.4 us (3%)
  other arithmetic  14.9 us (3%)
    reduce_scatter x1, waiting for transfers between devices, local(): lax.psum_scatter(term_two, 'dp', scatter_dimension=1, tiled=True)  108 us
    psum x1, waiting for transfers between devices, local(): lax.psum((grad_gain_one, grad_gain_two, pulled[2], pulled[3], pulled[4],...  43.3 us
    psum x1, blocking collectives, local(): lax.psum((grad_gain_one, grad_gain_two, pulled[2], pulled[3], pulled[4],...  41.9 us
    reduce_scatter x1, waiting for transfers between devices, local(): lax.psum_scatter(term_one, 'dp', scatter_dimension=1, tiled=True)  33.6 us
    unnamed x7, waiting for transfers between devices  32.1 us
    unnamed x69, local copies, waits for them, and re-layouts  19.4 us
    dot_general x16, matrix products, meridian_apply(): return jnp.einsum('hk,bhmd->bkmd', table, field, precision=highest)  14.6 us
    all_to_all x1, waiting for transfers between devices, local(): lax.all_to_all(stash, 'space', split_axis=1, concat_axis=0, tiled=True)  12.9 us
  transfers between devices with their start and end apart: 14, of which 12 were waited for; matrix products, arithmetic and copies ran while one was open for 18% of the time, Pallas kernels for 0%

commit v1 on v0

--- a/solution.py
+++ b/solution.py
@@ -170,17 +170,20 @@
     bias_sum = jnp.sum(grad_hidden, axis=0)
     out_sum = jnp.sum(cotangent, axis=(0, 1, 2), dtype=jnp.float32)
     totals = lax.psum(
-        (
-            grad_gain_one,
-            grad_gain_two,
-            pulled[2],
-            pulled[3],
-            pulled[4],
-            pulled[5],
-            bias_sum,
-            out_sum,
+        lax.psum(
+            (
+                grad_gain_one,
+                grad_gain_two,
+                pulled[2],
+                pulled[3],
+                pulled[4],
+                pulled[5],
+                bias_sum,
+                out_sum,
+            ),
+            "space",
         ),
-        ("dp", "space"),
+        "dp",
     )
     paired = (
         lax.psum_scatter(term_one, "dp", scatter_dimension=1, tiled=True),

time: 549 us -> 665 us (1.21)
  waiting for transfers between devices: 294 us -> 376 us
  blocking collectives: 41.9 us -> 68.1 us
    unnamed x7 -> x8, waiting for transfers between devices: 32.1 us -> 81.3 us
    psum x1, waiting for transfers between devices: 43.3 us -> 77.4 us  [local(): lax.psum((grad_gain_one, grad_gain_two, pulled[2], pulled[3], pulled[4],...]
    psum x1, blocking collectives: 41.9 us -> 60.4 us  [local(): lax.psum((grad_gain_one, grad_gain_two, pulled[2], pulled[3], pulled[4],...]
    all_to_all x1, waiting for transfers between devices: 0.01 us -> 11.7 us  [local(): lax.all_to_all(grad_merid_real, 'space', split_axis=1, concat_axis=2, til...]
    reduce_scatter x1, waiting for transfers between devices: 33.6 us -> 22 us  [local(): lax.psum_scatter(term_one, 'dp', scatter_dimension=1, tiled=True)]
    psum x0 -> x1, blocking collectives: none -> 7.74 us  [local(): lax.psum(lax.psum((grad_gain_one, grad_gain_two, pulled[2], pulled[3], pu...]
    unnamed x69 -> x85, local copies, waits for them, and re-layouts: 19.4 us -> 21 us
  transfers between devices with their start and end apart: 14 -> 15, of which waited for: 12 -> 14; matrix products, arithmetic and copies ran while one was open for 18% -> 11% of each run, Pallas kernels for 0% -> 0%
where the time goes in v1:
time: 665 us; the launch traced here: 657 us
  waiting for transfers between devices  376 us (57%)
  matrix products  93.2 us (14%)
  blocking collectives  68.1 us (10%)
  local copies, waits for them, and re-layouts  45.9 us (7%)
  starting transfers between devices  40.3 us (6%)
  between operations  17.1 us (3%)
  other arithmetic  16 us (2%)
    reduce_scatter x1, waiting for transfers between devices, local(): lax.psum_scatter(term_two, 'dp', scatter_dimension=1, tiled=True)  106 us
    unnamed x8, waiting for transfers between devices  81.3 us
    psum x1, waiting for transfers between devices, local(): lax.psum((grad_gain_one, grad_gain_two, pulled[2], pulled[3], pulled[4],...  77.4 us
    psum x1, blocking collectives, local(): lax.psum((grad_gain_one, grad_gain_two, pulled[2], pulled[3], pulled[4],...  60.4 us
    reduce_scatter x1, waiting for transfers between devices, local(): lax.psum_scatter(term_one, 'dp', scatter_dimension=1, tiled=True)  22 us
    unnamed x85, local copies, waits for them, and re-layouts  21 us
    dot_general x16, matrix products, meridian_apply(): return jnp.einsum('hk,bhmd->bkmd', table, field, precision=highest)  15.4 us
  transfers between devices with their start and end apart: 15, of which 14 were waited for; matrix products, arithmetic and copies ran while one was open for 11% of the time, Pallas kernels for 0%

profile of v1, /device:TPU:0, one launch (start us, length us, event | category | flops | bytes accessed | tf_op | source)
XLA Modules:
  0.0 656.5 jit_solution(1905161802765140276)
XLA Ops:
  8.0 7.4 %all-to-all-start = ((bf16[1,16,2,8640]{3,2,0,1:T(2,128)(2,1)}), bf16[1,16,2,8640]{3,2,0,1:T(2,128)(2,1)S(1)}, u32[]{:S(2)}, u32[]{:S(2)}) async-start(bf16[1,16,2,8640]{3,2,0,1:T(2,128)(2,1)} %bitcast.441), calls=%async_computation | async-start | bytes 1114112 | tf_op jit(solution)/shard_map/all_to_all | solution.py:102
  15.5 1.9 sort.17
  17.4 12.9 %all-to-all-done = bf16[1,16,2,8640]{3,2,0,1:T(2,128)(2,1)S(1)} async-done(((bf16[1,16,2,8640]{3,2,0,1:T(2,128)(2,1)}), bf16[1,16,2,8640]{3,2,0,1:T(2,128)(2,1)S(1)}, u32[]{:S(2)}, u32[]{:S(2)}) %all-to-all-start) | async-done | bytes 552992 | tf_op jit(solution)/shard_map/all_to_all | solution.py:102
  30.2 1.7 gather_fusion
  34.9 1.2 convolution_bitcast_fusion.4
  37.2 4.3 all-to-all-start.1
  41.6 1.3 fusion.29
  43.9 9.8 %all-to-all-done.1 = f32[2,1,64,768]{3,0,1,2:T(2,128)S(1)} async-done(((f32[2,1,64,768]{3,0,1,2:T(2,128)}), f32[2,1,64,768]{3,0,1,2:T(2,128)S(1)}, u32[]{:S(2)}, u32[]{:S(2)}) %all-to-all-start.1) | async-done | bytes 393248 | tf_op jit(solution)/shard_map/all_to_all | solution.py:116
  53.7 3.8 all-to-all-start.2
  57.9 1.3 fusion.143
  59.2 10.4 %all-to-all-done.2 = f32[2,1,64,768]{3,0,1,2:T(2,128)S(1)} async-done(((f32[2,1,64,768]{3,0,1,2:T(2,128)}), f32[2,1,64,768]{3,0,1,2:T(2,128)S(1)}, u32[]{:S(2)}, u32[]{:S(2)}) %all-to-all-start.2) | async-done | bytes 393248 | tf_op jit(solution)/shard_map/all_to_all | solution.py:117
  69.6 1.3 fusion.139
  71.0 1.7 fusion.28
  73.6 1.5 fusion.106
  75.1 1.3 fusion.27
  76.4 1.3 reshape.375
  79.8 1.6 fusion.111
  84.0 1.8 fusion.19
  88.4 3.6 all-to-all-start.3
  95.1 9.1 %all-to-all-done.3 = f32[2,16,4,768]{3,2,0,1:T(4,128)S(1)} async-done(((f32[2,16,4,768]{3,2,0,1:T(4,128)}), f32[2,16,4,768]{3,2,0,1:T(4,128)S(1)}, u32[]{:S(2)}, u32[]{:S(2)}) %all-to-all-start.3) | async-done | bytes 393248 | tf_op jit(solution)/shard_map/all_to_all | solution.py:125
  104.1 4.0 all-to-all-start.4
  108.2 6.4 fusion.368
  114.7 1.3 fusion.131
  116.1 4.2 all-to-all-done.4
  120.5 1.6 fusion.365
  123.5 9.5 %fusion.363 = (f32[3072]{0:T(1024)S(1)}, bf16[360,3072]{1,0:T(8,128)(2,1)S(1)}, f32[360,3072]{1,0:T(8,128)}) fusion(f32[360,3072]{1,0:T(8,128)} %fusion.368, f32[3072]{0:T(1024)S(1)} %copy-done.38, bf16[360,768]{1,0:T(8,128)(2,1)S(1)} %reshape.380, bf16[768,3072]{1,0:T(8,128)(2,1)} %param.20), kind=kOutput, calls=%fused_computation.455 | convolution fusion | flops 1723020288 | bytes 16355328 | tf_op jit(solution)/shard_map/dot_general | solution.py:132
  133.0 1.3 copy-done.20
  134.4 5.2 fusion.34
  139.6 1.4 reshape.381
  143.1 1.7 convert_reduce_fusion
  146.9 3.6 all-to-all-start.5
  152.6 10.0 %all-to-all-done.5 = f32[2,1,64,768]{3,0,1,2:T(2,128)S(1)} async-done(((f32[2,1,64,768]{3,0,1,2:T(2,128)}), f32[2,1,64,768]{3,0,1,2:T(2,128)S(1)}, u32[]{:S(2)}, u32[]{:S(2)}) %all-to-all-start.5) | async-done | bytes 393248 | tf_op jit(solution)/shard_map/all_to_all | solution.py:152
  162.6 3.6 all-to-all-start.6
  166.4 1.3 fusion.137
  167.7 10.6 %all-to-all-done.6 = f32[2,1,64,768]{3,0,1,2:T(2,128)S(1)} async-done(((f32[2,1,64,768]{3,0,1,2:T(2,128)}), f32[2,1,64,768]{3,0,1,2:T(2,128)S(1)}, u32[]{:S(2)}, u32[]{:S(2)}) %all-to-all-start.6) | async-done | bytes 393248 | tf_op jit(solution)/shard_map/all_to_all | solution.py:151
  178.3 1.3 fusion.133
  179.6 1.6 fusion.367
  181.5 2.8 fusion.85
  184.4 1.6 fusion.87
  186.0 1.3 fusion.366
  187.4 2.0 reshape.384
  189.4 2.5 fusion.61
  198.5 1.2 convolution_bitcast_fusion.10
  203.2 1.4 pad_add_fusion
  205.7 6.7 %fusion.32 = f32[768,3072]{1,0:T(8,128)} fusion(bf16[360,768]{1,0:T(8,128)(2,1)S(1)} %copy-done.24, bf16[360,3072]{1,0:T(8,128)(2,1)} %copy-done.20), kind=kOutput, calls=%fused_computation.84 | convolution fusion | flops 1698693120 | bytes 12201984 | tf_op jit(solution)/shard_map/td,tf->df/dot_general | solution.py:142
  213.4 8.9 %convolution_bitcast_fusion = f32[768,3072]{0,1:T(8,128)} fusion(bf16[360,768]{1,0:T(8,128)(2,1)S(1)} %copy-done.32, f32[360,3072]{1,0:T(8,128)} %get-tuple-element.91), kind=kOutput, calls=%fused_computation.3 | convolution fusion | flops 1708646400 | bytes 14413824 | tf_op jit(solution)/shard_map/td,tf->df/dot_general | solution.py:145
  222.4 77.4 %all-reduce.19.cloned.1.call-done = (f32[2,8,96,96]{3,2,1,0:T(8,128)}, f32[2,8,96,96]{3,2,1,0:T(8,128)}) async-done(((f32[2,8,96,96]{3,2,1,0:T(8,128)}, f32[2,8,96,96]{3,2,1,0:T(8,128)}), (f32[2,8,96,96]{3,2,1,0:T(8,128)}, f32[2,8,96,96]{3,2,1,0:T(8,128)})) %all-reduce.19.cloned.1.call-update) | async-done | bytes 1179664 | tf_op jit(solution)/shard_map/psum | solution.py:173
  299.8 22.0 %reduce-scatter.9.cloned.1.call-done = f32[768,1536]{1,0:T(8,128)} async-done(((f32[768,3072]{1,0:T(8,128)}), f32[768,1536]{1,0:T(8,128)}) %reduce-scatter.9.cloned.1.call-update) | async-done | bytes 4718608 | tf_op jit(solution)/shard_map/reduce_scatter | solution.py:189
  321.8 6.1 copy.208
  328.2 106.4 %reduce-scatter.11.cloned.1.call-done = f32[768,1536]{0,1:T(8,128)} async-done(((f32[768,3072]{0,1:T(8,128)}), f32[768,1536]{0,1:T(8,128)}) %reduce-scatter.11.cloned.1.call-update) | async-done | bytes 4718608 | tf_op jit(solution)/shard_map/reduce_scatter | solution.py:190
  435.7 1.9 fusion.124
  440.9 1.9 fusion.118
  448.1 5.6 all-to-all-start.8
  455.7 10.1 %all-to-all-done.8 = f32[2,16,4,768]{3,2,0,1:T(4,128)S(1)} async-done(((f32[2,16,4,768]{3,2,0,1:T(4,128)}), f32[2,16,4,768]{3,2,0,1:T(4,128)S(1)}, u32[]{:S(2)}, u32[]{:S(2)}) %all-to-all-start.8) | async-done | bytes 393248 | tf_op jit(solution)/shard_map/all_to_all | solution.py:161
  465.8 3.8 all-to-all-start.7
  470.1 11.7 %all-to-all-done.7 = f32[2,16,4,768]{3,2,0,1:T(4,128)S(1)} async-done(((f32[2,16,4,768]{3,2,0,1:T(4,128)}), f32[2,16,4,768]{3,2,0,1:T(4,128)S(1)}, u32[]{:S(2)}, u32[]{:S(2)}) %all-to-all-start.7) | async-done | bytes 393248 | tf_op jit(solution)/shard_map/all_to_all | solution.py:160
  482.0 1.3 convolution_bitcast_fusion.1
  483.4 1.7 multiply_reduce_fusion.2
  486.1 2.1 copy.188
  488.2 60.4 %all-reduce.12 = (f32[3072]{0:T(1024)S(1)}, f32[768]{0:T(1024)S(1)}, f32[768]{0:T(1024)S(1)}, f32[768]{0:T(1024)S(1)}, f32[2,768]{1,0:T(2,128)S(1)}, /*index=5*/f32[2,768]{1,0:T(2,128)S(1)}) all-reduce(f32[3072]{0:T(1024)S(1)} %get-tuple-element.81, f32[768]{0:T(1024)S(1)} %get-tuple-element.83, ...), channel_id=1, replica_groups=mesh['dp'=2,'space'=16] {'space'}, use_global_device_ids=true, to_apply=%region_14.15 | all-reduce | flops 8448 | bytes 67584 | tf_op jit(solution)/shard_map/psum | solution.py:173
  548.6 7.7 %all-reduce.14 = (f32[3072]{0:T(1024)S(1)}, f32[768]{0:T(1024)S(1)}, f32[768]{0:T(1024)S(1)}, f32[768]{0:T(1024)S(1)}, f32[2,768]{1,0:T(2,128)S(1)}, /*index=5*/f32[2,768]{1,0:T(2,128)S(1)}) all-reduce(f32[3072]{0:T(1024)S(1)} %get-tuple-element.65, f32[768]{0:T(1024)S(1)} %get-tuple-element.66, ...), channel_id=1, replica_groups=mesh['dp'=2,'space'=16] {'dp'}, use_global_device_ids=true, to_apply=%region_15.16 | all-reduce | flops 8448 | bytes 67584 | tf_op jit(solution)/shard_map/psum | solution.py:172
  560.0 2.2 broadcast_multiply_fusion.1
  563.1 4.9 reduce-scatter.13.cloned.1.call-done
  570.1 76.3 %reduce-scatter.15.cloned.1.call-done = f32[96,768]{1,0:T(8,128)} async-done(((f32[1536,768]{1,0:T(8,128)}), f32[96,768]{1,0:T(8,128)}) %reduce-scatter.15.cloned.1.call-update) | async-done | bytes 294928
  (191 shorter events, 59.4 us)
Async XLA Ops:
  8.0 22.2 %all-to-all-start = ((bf16[1,16,2,8640]{3,2,0,1:T(2,128)(2,1)}), bf16[1,16,2,8640]{3,2,0,1:T(2,128)(2,1)S(1)}, u32[]{:S(2)}, u32[]{:S(2)}) async-start(bf16[1,16,2,8640]{3,2,0,1:T(2,128)(2,1)} %bitcast.441), calls=%async_computation | async-start | bytes 1114112 | tf_op jit(solution)/shard_map/all_to_all | solution.py:102
  34.3 0.7 copy-start.34
  37.2 16.5 %all-to-all-start.1 = ((f32[2,1,64,768]{3,0,1,2:T(2,128)}), f32[2,1,64,768]{3,0,1,2:T(2,128)S(1)}, u32[]{:S(2)}, u32[]{:S(2)}) async-start(f32[2,1,64,768]{3,0,1,2:T(2,128)} %copy.140), calls=%async_computation.1 | async-start | bytes 786432 | tf_op jit(solution)/shard_map/all_to_all | solution.py:116
  42.8 14.7 %copy-start.36 = (f32[2,768]{1,0:T(2,128)S(1)}, f32[2,768]{1,0:T(2,128)}, u32[]{:S(2)}) copy-start(f32[2,768]{1,0:T(2,128)} %param.16) | copy-start | bytes 18436
  42.9 14.9 %copy-start.37 = (f32[2,768]{1,0:T(2,128)S(1)}, f32[2,768]{1,0:T(2,128)}, u32[]{:S(2)}) copy-start(f32[2,768]{1,0:T(2,128)} %param.18) | copy-start | bytes 18436
  53.7 15.9 %all-to-all-start.2 = ((f32[2,1,64,768]{3,0,1,2:T(2,128)}), f32[2,1,64,768]{3,0,1,2:T(2,128)S(1)}, u32[]{:S(2)}, u32[]{:S(2)}) async-start(f32[2,1,64,768]{3,0,1,2:T(2,128)} %copy.142), calls=%async_computation.2 | async-start | bytes 786432 | tf_op jit(solution)/shard_map/all_to_all | solution.py:117
  71.0 1.9 copy-start.5
  72.9 2.1 copy-start.1
  72.9 2.1 copy-start.29
  76.4 1.3 copy-start.27
  77.7 3.7 copy-start.3
  77.7 1.3 copy-start.16
  79.0 2.4 copy-start.25
  82.1 1.3 copy-start.7
  82.9 1.1 copy-start.17
  86.9 5.1 copy-start.21
  88.4 15.7 %all-to-all-start.3 = ((f32[2,16,4,768]{3,2,0,1:T(4,128)}), f32[2,16,4,768]{3,2,0,1:T(4,128)S(1)}, u32[]{:S(2)}, u32[]{:S(2)}) async-start(f32[2,16,4,768]{3,2,0,1:T(4,128)} %copy.152), calls=%async_computation.3 | async-start | bytes 786432 | tf_op jit(solution)/shard_map/all_to_all | solution.py:125
  94.1 14.1 %copy-start.31 = (bf16[360,768]{1,0:T(8,128)(2,1)S(1)}, bf16[360,768]{1,0:T(8,128)(2,1)}, u32[]{:S(2)}) copy-start(bf16[360,768]{1,0:T(8,128)(2,1)} %reshape.373) | copy-start | bytes 1658884
  104.1 16.1 %all-to-all-start.4 = ((f32[2,16,4,768]{3,2,0,1:T(4,128)}), f32[2,16,4,768]{3,2,0,1:T(4,128)S(1)}, u32[]{:S(2)}, u32[]{:S(2)}) async-start(f32[2,16,4,768]{3,2,0,1:T(4,128)} %copy.155), calls=%async_computation.4 | async-start | bytes 786432 | tf_op jit(solution)/shard_map/all_to_all | solution.py:126
  122.1 0.7 copy-start.35
  122.8 0.7 copy-start.38
  123.5 9.5 %copy-start.23 = (bf16[360,768]{1,0:T(8,128)(2,1)}, bf16[360,768]{1,0:T(8,128)(2,1)S(1)}, u32[]{:S(2)}) copy-start(bf16[360,768]{1,0:T(8,128)(2,1)S(1)} %reshape.380) | copy-start | bytes 1658884
  133.0 1.3 copy-start.20
  141.0 1.0 copy-start
  142.0 1.1 copy-start.22
  146.9 15.7 %all-to-all-start.5 = ((f32[2,1,64,768]{3,0,1,2:T(2,128)}), f32[2,1,64,768]{3,0,1,2:T(2,128)S(1)}, u32[]{:S(2)}, u32[]{:S(2)}) async-start(f32[2,1,64,768]{3,0,1,2:T(2,128)} %copy.158), calls=%async_computation.5 | async-start | bytes 786432 | tf_op jit(solution)/shard_map/all_to_all | solution.py:152
  162.6 17.0 %copy-start.14 = (f32[2,1,64,768]{3,0,1,2:T(2,128)}, f32[2,1,64,768]{3,0,1,2:T(2,128)S(1)}, u32[]{:S(2)}) copy-start(f32[2,1,64,768]{3,0,1,2:T(2,128)S(1)} %all-to-all-done.5) | copy-start | bytes 1179652
  162.6 15.7 %all-to-all-start.6 = ((f32[2,1,64,768]{3,0,1,2:T(2,128)}), f32[2,1,64,768]{3,0,1,2:T(2,128)S(1)}, u32[]{:S(2)}, u32[]{:S(2)}) async-start(f32[2,1,64,768]{3,0,1,2:T(2,128)} %copy.160), calls=%async_computation.6 | async-start | bytes 786432 | tf_op jit(solution)/shard_map/all_to_all | solution.py:151
  166.2 133.6 %all-reduce.19.cloned.1.call-start = ((), (), s32[]{:S(2)}) async-start(), calls=%async_computation.17 | async-start | bytes 3145728 | tf_op jit(solution)/shard_map/psum | solution.py:173
  181.5 2.9 copy-start.18
  181.5 4.5 copy-start.15
  181.5 4.5 copy-start.28
  186.0 3.4 copy-start.8
  191.9 4.4 copy-start.9
  191.9 1.2 copy-start.13
  193.2 2.1 copy-start.2
  194.2 2.1 copy-start.4
  195.2 2.1 copy-start.19
  195.2 2.1 copy-start.26
  195.3 2.1 copy-start.33
  198.5 2.3 copy-start.10
  204.6 1.1 copy-start.24
  204.6 117.2 %reduce-scatter.9.cloned.1.call-start = ((), (), s32[]{:S(2)}) async-start(), calls=%async_computation.13 | async-start | bytes 14155776 | tf_op jit(solution)/shard_map/reduce_scatter | solution.py:189
  212.3 1.1 copy-start.32
  212.4 222.2 %reduce-scatter.11.cloned.1.call-start = ((), (), s32[]{:S(2)}) async-start(), calls=%async_computation.14 | async-start | bytes 14155776 | tf_op jit(solution)/shard_map/reduce_scatter | solution.py:190
  222.3 337.6 %all-reduce.21.cloned.1.call-start = ((), (), s32[]{:S(2)}) async-start(), calls=%async_computation.18 | async-start | bytes 3145728 | tf_op jit(solution)/shard_map/psum | solution.py:172
  299.8 268.2 %reduce-scatter.13.cloned.1.call-start = ((), (), s32[]{:S(2)}) async-start(), calls=%async_computation.15 | async-start | bytes 5013504
  327.9 318.5 %reduce-scatter.15.cloned.1.call-start = ((), (), s32[]{:S(2)}) async-start(), calls=%async_computation.16 | async-start | bytes 5013504
  434.6 1.1 copy-start.6
  435.7 1.9 copy-start.11
  440.9 1.9 copy-start.12
  448.1 17.8 %all-to-all-start.8 = ((f32[2,16,4,768]{3,2,0,1:T(4,128)}), f32[2,16,4,768]{3,2,0,1:T(4,128)S(1)}, u32[]{:S(2)}, u32[]{:S(2)}) async-start(f32[2,16,4,768]{3,2,0,1:T(4,128)} %copy.176), calls=%async_computation.8 | async-start | bytes 786432 | tf_op jit(solution)/shard_map/all_to_all | solution.py:161
  465.8 16.0 %all-to-all-start.7 = ((f32[2,16,4,768]{3,2,0,1:T(4,128)}), f32[2,16,4,768]{3,2,0,1:T(4,128)S(1)}, u32[]{:S(2)}, u32[]{:S(2)}) async-start(f32[2,16,4,768]{3,2,0,1:T(4,128)} %copy.173), calls=%async_computation.7 | async-start | bytes 786432 | tf_op jit(solution)/shard_map/all_to_all | solution.py:160
  560.0 2.2 copy-start.30
Sparse Core Ops, SparseCore 0:
  204.8 94.9 all-reduce.18
Sparse Core Ops, SparseCore 1:
  212.4 109.3 reduce-scatter.8
  324.0 110.6 reduce-scatter.10
  436.8 51.3 all-reduce.20
  492.1 75.9 reduce-scatter.12
  571.9 74.4 reduce-scatter.14
